TPU v7x, 32 devices: a whole 2x2x4 slice. The times are simulated.
32 devices in a mesh: tau: 2 (over y), aux: 16 (over z, x, core).
Axes of the slice: x: 2, y: 2, z: 4, core: 2. Of those that a mesh axis runs over, the one named last changes fastest.
Arguments:
- coefficients: bfloat16 [16384, 2048], P('aux'), may hold values from -0.125 to 0.125
- green_occ: bfloat16 [16, 2048, 2048], P('tau', 'aux'), may hold values from -6 to 6
- green_vir: bfloat16 [16, 2048, 2048], P('tau', 'aux'), may hold values from -6 to 6
- minimax: float32 [16, 16], replicated, may hold values from -1.5 to 1.5
- coulomb: float32 [512], replicated, may hold values from 0.006 to 0.04
Outputs:
- screened: float32 [16, 16384, 512], P('tau', 'aux')
All inputs are finite; a program needn't handle non-finite values.
Results may differ from a plain program's by a relative error of at most 0.0078.
Values may be sent and summed in bfloat16 or wider, within the bound.
No kernel may reach another device: no remote copies, remote signals or barrier semaphores. Data moves between devices by JAX's collectives and lax.ppermute only.
A program may use at most 128 MiB of HBM per device.

v0:
```python
import jax
import jax.numpy as jnp
from jax import lax
from jax.sharding import PartitionSpec as P

NAUX = 16384
PANEL = 512
DYSON = 4


def per_device(coefficients, green_occ, green_vir, minimax, coulomb):
    stride = NAUX // PANEL
    local_panel = coefficients[::stride]
    panel_coef = lax.all_gather(local_panel, "aux", axis=0, tiled=True)
    product = (green_occ.astype(jnp.float32) * green_vir.astype(jnp.float32)).astype(jnp.bfloat16)
    folded = jnp.einsum(
        "tkn,qn->tkq", product, panel_coef, preferred_element_type=jnp.float32
    ).astype(jnp.bfloat16)
    owners = lax.axis_size("tau")
    freq_count = minimax.shape[0] // owners
    own_rows = lax.dynamic_slice_in_dim(minimax, lax.axis_index("tau") * freq_count, freq_count, 0)
    gathered = lax.all_gather(folded, "tau", axis=0, tiled=True)
    mixed = jnp.einsum(
        "wt,tkq->wkq", own_rows, gathered.astype(jnp.float32), precision=lax.Precision.HIGHEST
    )
    wide_coef = coefficients.astype(jnp.float32)
    chi_freq = jnp.einsum(
        "pk,wkq->wpq",
        wide_coef,
        lax.all_gather(mixed, "aux", axis=1, tiled=True),
        precision=lax.Precision.HIGHEST,
    )
    coupling = lax.all_gather(chi_freq[:, ::stride, :], "aux", axis=1, tiled=True)
    screened = chi_freq
    for sweep in range(DYSON):
        screened = chi_freq + jnp.einsum(
            "wpq,wqr->wpr", screened * coulomb, coupling, precision=lax.Precision.HIGHEST
        )
    return screened


def solution(mesh):
    placed = (P("aux", None), P("tau", "aux", None), P("tau", "aux", None), P(), P())
    return jax.shard_map(
        per_device, mesh=mesh, in_specs=placed, out_specs=P("tau", "aux", None), check_vma=False
    )
```

profile of v0, /device:TPU:0, one launch (start us, length us, event | category | flops | bytes accessed | tf_op | source)
XLA Modules:
  0.0 695.1 jit_solution(247652757352555016)
XLA Ops:
  6.5 0.0 copy-start
  6.5 0.0 all-gather.5.cloned.1.call-start
  6.5 3.0 slice.6
  9.5 0.0 all-gather.5.cloned.1.call-update
  9.5 0.0 all-gather.7.cloned.1.call-start
  9.6 44.3 %all-gather.5.cloned.1.call-done = bf16[512,2048]{1,0:T(8,128)(2,1)} async-done(((bf16[32,2048]{1,0:T(8,128)(2,1)}), bf16[512,2048]{1,0:T(8,128)(2,1)}) %all-gather.5.cloned.1.call-update) | async-done | bytes 2097168 | tf_op jit(solution)/shard_map/all_gather | solution.py:14
  53.9 7.4 %fusion.27 = bf16[8,128,512]{2,1,0:T(8,128)(2,1)} fusion(bf16[512,2048]{1,0:T(8,128)(2,1)} %all-gather.5.cloned.1.call-done, bf16[8,128,2048]{2,1,0:T(8,128)(2,1)} %param.7, bf16[8,128,2048]{2,1,0:T(8,128)(2,1)} %param.6), kind=kOutput, calls=%fused_computation.27 | convolution fusion | flops 2156396544 | bytes 11534336 | tf_op jit(solution)/shard_map/tkn,qn->tkq/dot_general | solution.py:16
  61.3 0.0 all-gather.7.cloned.1.call-update
  61.3 0.0 all-gather.9.cloned.1.call-start
  61.3 31.9 %all-gather.7.cloned.1.call-done = bf16[16,128,512]{2,1,0:T(8,128)(2,1)} async-done(((bf16[8,128,512]{2,1,0:T(8,128)(2,1)}), bf16[16,128,512]{2,1,0:T(8,128)(2,1)}) %all-gather.7.cloned.1.call-update) | async-done | bytes 2097168 | tf_op jit(solution)/shard_map/all_gather | solution.py:22
  93.3 0.0 copy-done
  93.3 3.5 fusion.25
  96.7 1.9 copy.16
  98.6 0.0 all-gather.9.cloned.1.call-update
  98.6 0.0 copy-start.3
  98.7 0.3 all-gather.11.cloned.1.call-start
  98.9 175.6 %all-gather.9.cloned.1.call-done = f32[8,2048,512]{1,2,0:T(8,128)} async-done(((f32[8,128,512]{1,2,0:T(8,128)}), f32[8,2048,512]{1,2,0:T(8,128)}) %all-gather.9.cloned.1.call-update) | async-done | bytes 33554448 | tf_op jit(solution)/shard_map/all_gather | solution.py:30
  274.5 59.4 %convolution_bitcast_fusion = f32[8,1024,512]{1,2,0:T(8,128)} fusion(f32[8,2048,512]{1,2,0:T(8,128)} %all-gather.9.cloned.1.call-done, bf16[1024,2048]{1,0:T(8,128)(2,1)} %param.5), kind=kOutput, calls=%fused_computation.12 | convolution fusion | flops 103079215104 | bytes 54525952 | tf_op jit(solution)/shard_map/pk,wkq->wpq/dot_general | solution.py:27
  333.9 27.1 %slice.7 = f32[8,32,512]{1,2,0:T(8,128)S(1)} slice(f32[8,1024,512]{1,2,0:T(8,128)} %convolution_bitcast_fusion), slice={[0:8:1], [0:1024:32], [0:512:1]} | slice | bytes 1048576 | tf_op jit(solution)/shard_map/slice | solution.py:33
  361.1 1.4 copy.10
  362.5 0.0 all-gather.11.cloned.1.call-update
  362.5 72.2 %all-gather.11.cloned.1.call-done = f32[8,512,512]{2,0,1:T(8,128)} async-done(((f32[8,32,512]{2,0,1:T(8,128)}), f32[8,512,512]{2,0,1:T(8,128)}) %all-gather.11.cloned.1.call-update) | async-done | bytes 8388624 | tf_op jit(solution)/shard_map/all_gather | solution.py:33
  434.8 0.0 copy-done.3
  434.8 0.0 copy-start.2
  434.8 75.6 %fusion.9 = f32[8,1024,512]{1,2,0:T(8,128)} fusion(f32[8,1024,512]{1,2,0:T(8,128)} %convolution_bitcast_fusion, f32[512]{0:T(512)S(1)} %copy-done.3, f32[8,512,512]{2,0,1:T(8,128)} %all-gather.11.cloned.1.call-done), kind=kOutput, calls=%fused_computation.9 | convolution fusion | flops 25773998080 | bytes 41945088 | tf_op jit(solution)/shard_map/wpq,wqr->wpr/dot_general | solution.py:36
  510.4 0.0 copy-done.2
  510.4 41.5 %fusion.6 = f32[8,1024,512]{1,2,0:T(8,128)} fusion(f32[8,1024,512]{1,2,0:T(8,128)} %convolution_bitcast_fusion, f32[8,1024,512]{1,2,0:T(8,128)} %fusion.9, f32[512]{0:T(512)S(1)} %copy-done.3, f32[8,512,512]{2,0,1:T(8,128)S(1)} %copy-done.2), kind=kOutput, calls=%fused_computation.6 | convolution fusion | flops 25778192384 | bytes 58722304 | tf_op jit(solution)/shard_map/wpq,wqr->wpr/dot_general | solution.py:36
  551.9 41.5 %fusion.3 = f32[8,1024,512]{1,2,0:T(8,128)} fusion(f32[8,1024,512]{1,2,0:T(8,128)} %convolution_bitcast_fusion, f32[8,1024,512]{1,2,0:T(8,128)} %fusion.6, f32[512]{0:T(512)S(1)} %copy-done.3, f32[8,512,512]{2,0,1:T(8,128)S(1)} %copy-done.2), kind=kOutput, calls=%fused_computation.3 | convolution fusion | flops 25778192384 | bytes 58722304 | tf_op jit(solution)/shard_map/wpq,wqr->wpr/dot_general | solution.py:36
  593.3 78.4 %fusion.11 = f32[8,1024,512]{1,2,0:T(8,128)} fusion(f32[8,1024,512]{1,2,0:T(8,128)} %convolution_bitcast_fusion, f32[8,1024,512]{1,2,0:T(8,128)} %fusion.3, f32[512]{0:T(512)S(1)} %copy-done.3, f32[8,512,512]{2,0,1:T(8,128)} %all-gather.11.cloned.1.call-done), kind=kOutput, calls=%fused_computation.11 | convolution fusion | flops 25782386688 | bytes 58722304 | tf_op jit(solution)/shard_map/wpq,wqr->wpr/dot_general | solution.py:36
  671.7 0.0 copy-start.1
  671.7 16.4 %copy.14 = f32[8,1024,512]{2,1,0:T(8,128)} copy(f32[8,1024,512]{1,2,0:T(8,128)} %fusion.11) | data formatting | bytes 33554432 | tf_op jit(solution)/shard_map/add | solution.py:36
  688.2 0.0 copy-done.1
Async XLA Ops:
  6.5 86.7 %copy-start = (f32[16,16]{1,0:T(8,128)S(1)}, f32[16,16]{1,0:T(8,128)}, u32[]{:S(2)}) copy-start(f32[16,16]{1,0:T(8,128)} %param.8) | copy-start | bytes 3076
  6.5 47.3 %all-gather.5.cloned.1.call-start = ((), (), s32[]{:S(2)}) async-start(), calls=%async_computation | async-start | bytes 2228224 | tf_op jit(solution)/shard_map/all_gather | solution.py:14
  9.5 83.7 %all-gather.7.cloned.1.call-start = ((), (), s32[]{:S(2)}) async-start(), calls=%async_computation.1 | async-start | bytes 3145728 | tf_op jit(solution)/shard_map/all_gather | solution.py:22
  61.3 213.2 %all-gather.9.cloned.1.call-start = ((), (), s32[]{:S(2)}) async-start(), calls=%async_computation.2 | async-start | bytes 35651584 | tf_op jit(solution)/shard_map/all_gather | solution.py:30
  98.6 336.1 %copy-start.3 = (f32[512]{0:T(512)S(1)}, f32[512]{0:T(512)}, u32[]{:S(2)}) copy-start(f32[512]{0:T(512)} %param.9) | copy-start | bytes 6148
  98.7 336.1 %all-gather.11.cloned.1.call-start = ((), (), s32[]{:S(2)}) async-start(), calls=%async_computation.3 | async-start | bytes 8912896 | tf_op jit(solution)/shard_map/all_gather | solution.py:33
  434.8 75.6 %copy-start.2 = (f32[8,512,512]{2,0,1:T(8,128)S(1)}, f32[8,512,512]{2,0,1:T(8,128)}, u32[]{:S(2)}) copy-start(f32[8,512,512]{2,0,1:T(8,128)} %all-gather.11.cloned.1.call-done) | copy-start | bytes 25165828
  671.7 16.4 %copy-start.1 = (f32[16,16]{1,0:T(8,128)S(1)}, f32[16,16]{1,0:T(8,128)}, u32[]{:S(2)}) copy-start(f32[16,16]{1,0:T(8,128)} %param.8) | copy-start | bytes 3076
Sparse Core Ops, SparseCore 0:
  9.7 44.1 all-gather.4
  61.4 31.8 all-gather.6
  98.8 175.7 all-gather.8
  362.7 72.0 all-gather.10
where the time goes:
time: 700 us; the launch traced here: 695 us
  waiting for transfers between devices  324 us (46%)
  matrix products  307 us (44%)
  local copies, waits for them, and re-layouts  49.8 us (7%)
  between operations  13.6 us (2%)
    dot_general x4, matrix products, per_device(): jnp.einsum('wpq,wqr->wpr', screened * coulomb, coupling, precision=lax.Pr...  237 us
    all_gather x1, waiting for transfers between devices, per_device(): lax.all_gather(mixed, 'aux', axis=1, tiled=True)  176 us
    all_gather x1, waiting for transfers between devices, per_device(): lax.all_gather(chi_freq[:, ::stride, :], 'aux', axis=1, tiled=True)  72.2 us
    dot_general x1, matrix products, per_device(): jnp.einsum('pk,wkq->wpq', wide_coef, lax.all_gather(mixed, 'aux', axis=1,...  59.4 us
    all_gather x1, waiting for transfers between devices, per_device(): panel_coef = lax.all_gather(local_panel, 'aux', axis=0, tiled=True)  44.3 us
    all_gather x1, waiting for transfers between devices, per_device(): gathered = lax.all_gather(folded, 'tau', axis=0, tiled=True)  31.9 us
    slice x2, local copies, waits for them, and re-layouts, per_device(): chi_freq[:, ::stride, :]  28.6 us
    add x1, local copies, waits for them, and re-layouts, per_device(): chi_freq + jnp.einsum('wpq,wqr->wpr', screened * coulomb, coupling, preci...  16.4 us
  transfers between devices with their start and end apart: 4, of which 4 were waited for; matrix products, arithmetic and copies ran while one was open for 0% of the time, Pallas kernels for 0%

commit v1 on v0

--- a/solution.py
+++ b/solution.py
@@ -30,7 +30,9 @@
         lax.all_gather(mixed, "aux", axis=1, tiled=True),
         precision=lax.Precision.HIGHEST,
     )
-    coupling = lax.all_gather(chi_freq[:, ::stride, :], "aux", axis=1, tiled=True)
+    part = chi_freq[:, ::stride, :]
+    parts = lax.all_gather(part, "aux", axis=0, tiled=False)
+    coupling = jnp.concatenate(parts, axis=1)
     screened = chi_freq
     for sweep in range(DYSON):
         screened = chi_freq + jnp.einsum(

time: 700 us -> 672 us (0.960)
  matrix products: 307 us -> 267 us
  local copies, waits for them, and re-layouts: 49.8 us -> 61.4 us
    dot_general x4, matrix products: 237 us -> 197 us  [per_device(): jnp.einsum('wpq,wqr->wpr', screened * coulomb, coupling, precision=lax.Pr...]
    all_gather x0 -> x1, local copies, waits for them, and re-layouts: none -> 9.65 us  [per_device(): parts = lax.all_gather(part, 'aux', axis=0, tiled=False)]
where the time goes in v1:
time: 672 us; the launch traced here: 667 us
  waiting for transfers between devices  324 us (48%)
  matrix products  267 us (40%)
  local copies, waits for them, and re-layouts  61.4 us (9%)
  between operations  13.6 us (2%)
    dot_general x4, matrix products, per_device(): jnp.einsum('wpq,wqr->wpr', screened * coulomb, coupling, precision=lax.Pr...  197 us
    all_gather x1, waiting for transfers between devices, per_device(): lax.all_gather(mixed, 'aux', axis=1, tiled=True)  176 us
    all_gather x1, waiting for transfers between devices, per_device(): parts = lax.all_gather(part, 'aux', axis=0, tiled=False)  72.2 us
    dot_general x1, matrix products, per_device(): jnp.einsum('pk,wkq->wpq', wide_coef, lax.all_gather(mixed, 'aux', axis=1,...  59.4 us
    all_gather x1, waiting for transfers between devices, per_device(): panel_coef = lax.all_gather(local_panel, 'aux', axis=0, tiled=True)  44.3 us
    all_gather x1, waiting for transfers between devices, per_device(): gathered = lax.all_gather(folded, 'tau', axis=0, tiled=True)  31.9 us
    slice x2, local copies, waits for them, and re-layouts, per_device(): part = chi_freq[:, ::stride, :]  29 us
    add x1, local copies, waits for them, and re-layouts, per_device(): chi_freq + jnp.einsum('wpq,wqr->wpr', screened * coulomb, coupling, preci...  16.4 us
  transfers between devices with their start and end apart: 4, of which 4 were waited for; matrix products, arithmetic and copies ran while one was open for 0% of the time, Pallas kernels for 0%

profile of v1, /device:TPU:0, one launch (start us, length us, event | category | flops | bytes accessed | tf_op | source)
XLA Modules:
  0.0 666.7 jit_solution(2894668255691026430)
XLA Ops:
  6.5 0.0 copy-start
  6.5 0.0 all-gather.6.cloned.1.call-start
  6.5 3.0 slice.6
  9.5 0.0 all-gather.6.cloned.1.call-update
  9.5 0.0 all-gather.8.cloned.1.call-start
  9.6 44.3 %all-gather.6.cloned.1.call-done = bf16[512,2048]{1,0:T(8,128)(2,1)} async-done(((bf16[32,2048]{1,0:T(8,128)(2,1)}), bf16[512,2048]{1,0:T(8,128)(2,1)}) %all-gather.6.cloned.1.call-update) | async-done | bytes 2097168 | tf_op jit(solution)/shard_map/all_gather | solution.py:14
  53.9 7.4 %fusion.23 = bf16[8,128,512]{2,1,0:T(8,128)(2,1)} fusion(bf16[512,2048]{1,0:T(8,128)(2,1)} %all-gather.6.cloned.1.call-done, bf16[8,128,2048]{2,1,0:T(8,128)(2,1)} %param.7, bf16[8,128,2048]{2,1,0:T(8,128)(2,1)} %param.6), kind=kOutput, calls=%fused_computation.23 | convolution fusion | flops 2156396544 | bytes 11534336 | tf_op jit(solution)/shard_map/tkn,qn->tkq/dot_general | solution.py:16
  61.3 0.0 all-gather.8.cloned.1.call-update
  61.3 0.0 all-gather.10.cloned.1.call-start
  61.3 31.9 %all-gather.8.cloned.1.call-done = bf16[16,128,512]{2,1,0:T(8,128)(2,1)} async-done(((bf16[8,128,512]{2,1,0:T(8,128)(2,1)}), bf16[16,128,512]{2,1,0:T(8,128)(2,1)}) %all-gather.8.cloned.1.call-update) | async-done | bytes 2097168 | tf_op jit(solution)/shard_map/all_gather | solution.py:22
  93.3 0.0 copy-done
  93.3 3.5 fusion.21
  96.7 1.9 copy.16
  98.6 0.0 all-gather.10.cloned.1.call-update
  98.6 0.3 all-gather.12.cloned.1.call-start
  98.9 175.6 %all-gather.10.cloned.1.call-done = f32[8,2048,512]{1,2,0:T(8,128)} async-done(((f32[8,128,512]{1,2,0:T(8,128)}), f32[8,2048,512]{1,2,0:T(8,128)}) %all-gather.10.cloned.1.call-update) | async-done | bytes 33554448 | tf_op jit(solution)/shard_map/all_gather | solution.py:30
  274.5 59.4 %convolution_bitcast_fusion = f32[8,1024,512]{1,2,0:T(8,128)} fusion(f32[8,2048,512]{1,2,0:T(8,128)} %all-gather.10.cloned.1.call-done, bf16[1024,2048]{1,0:T(8,128)(2,1)} %param.5), kind=kOutput, calls=%fused_computation.12 | convolution fusion | flops 103079215104 | bytes 54525952 | tf_op jit(solution)/shard_map/pk,wkq->wpq/dot_general | solution.py:27
  333.9 0.0 copy-start.3
  333.9 27.5 %slice.7 = f32[8,32,512]{1,2,0:T(8,128)S(1)} slice(f32[8,1024,512]{1,2,0:T(8,128)} %convolution_bitcast_fusion), slice={[0:8:1], [0:1024:32], [0:512:1]} | slice | bytes 1048576 | tf_op jit(solution)/shard_map/slice | solution.py:33
  361.5 1.4 copy.10
  362.9 0.0 all-gather.12.cloned.1.call-update
  362.9 72.2 %all-gather.12.cloned.1.call-done = f32[128,32,512]{2,1,0:T(8,128)} async-done(((f32[8,32,512]{2,1,0:T(8,128)}), f32[128,32,512]{2,1,0:T(8,128)}) %all-gather.12.cloned.1.call-update) | async-done | bytes 8388624 | tf_op jit(solution)/shard_map/all_gather | solution.py:34
  435.2 0.0 copy-start.2
  435.2 9.7 %copy.11 = f32[16,8,32,512]{3,2,0,1:T(8,128)} copy(f32[16,8,32,512]{3,2,1,0:T(8,128)} %bitcast.28) | data formatting | bytes 16777216 | tf_op jit(solution)/shard_map/all_gather | solution.py:34
  444.8 0.0 copy-done.3
  444.8 1.5 copy-done.2
  446.3 0.0 slice-start
  446.3 32.8 %fusion.9 = f32[8,1024,512]{1,2,0:T(8,128)} fusion(f32[8,512,512]{2,1,0:T(8,128)} %bitcast.22, f32[8,1024,512]{1,2,0:T(8,128)S(1)} %copy-done.2, f32[512]{0:T(512)S(1)} %copy-done.3), kind=kOutput, calls=%fused_computation.9 | convolution fusion | flops 25773998080 | bytes 41945088 | tf_op jit(solution)/shard_map/wpq,wqr->wpr/dot_general | solution.py:38
  479.2 0.0 slice-start.1
  479.2 64.2 %fusion.6 = f32[8,1024,512]{1,2,0:T(8,128)} fusion(f32[8,512,512]{2,1,0:T(8,128)} %bitcast.23, f32[8,1024,512]{1,2,0:T(8,128)} %convolution_bitcast_fusion, f32[8,1024,512]{1,2,0:T(8,128)} %fusion.9, f32[512]{0:T(512)S(1)} %copy-done.3), kind=kOutput, calls=%fused_computation.6 | convolution fusion | flops 25778192384 | bytes 58722304 | tf_op jit(solution)/shard_map/wpq,wqr->wpr/dot_general | solution.py:38
  543.4 0.0 slice-done
  543.4 0.0 slice-done.1
  543.4 35.7 %fusion.3 = f32[8,1024,512]{1,2,0:T(8,128)} fusion(f32[8,512,512]{2,1,0:T(8,128)S(1)} %bitcast.27, f32[8,1024,512]{1,2,0:T(8,128)} %convolution_bitcast_fusion, f32[8,1024,512]{1,2,0:T(8,128)} %fusion.6, f32[512]{0:T(512)S(1)} %copy-done.3), kind=kOutput, calls=%fused_computation.3 | convolution fusion | flops 25778192384 | bytes 58722304 | tf_op jit(solution)/shard_map/wpq,wqr->wpr/dot_general | solution.py:38
  579.1 0.0 copy-start.1
  579.1 64.2 %fusion.11 = f32[8,1024,512]{1,2,0:T(8,128)} fusion(f32[8,1024,512]{1,2,0:T(8,128)} %convolution_bitcast_fusion, f32[8,512,512]{2,1,0:T(8,128)} %bitcast.24, f32[8,1024,512]{1,2,0:T(8,128)} %fusion.3, f32[512]{0:T(512)S(1)} %copy-done.3), kind=kOutput, calls=%fused_computation.11 | convolution fusion | flops 25782386688 | bytes 58722304 | tf_op jit(solution)/shard_map/wpq,wqr->wpr/dot_general | solution.py:38
  643.3 16.4 %copy.14 = f32[8,1024,512]{2,1,0:T(8,128)} copy(f32[8,1024,512]{1,2,0:T(8,128)} %fusion.11) | data formatting | bytes 33554432 | tf_op jit(solution)/shard_map/add | solution.py:38
  659.7 0.0 copy-done.1
  (1 shorter events, 0.0 us)
Async XLA Ops:
  6.5 86.7 %copy-start = (f32[16,16]{1,0:T(8,128)S(1)}, f32[16,16]{1,0:T(8,128)}, u32[]{:S(2)}) copy-start(f32[16,16]{1,0:T(8,128)} %param.8) | copy-start | bytes 3076
  6.5 47.3 %all-gather.6.cloned.1.call-start = ((), (), s32[]{:S(2)}) async-start(), calls=%async_computation | async-start | bytes 2228224 | tf_op jit(solution)/shard_map/all_gather | solution.py:14
  9.5 83.7 %all-gather.8.cloned.1.call-start = ((), (), s32[]{:S(2)}) async-start(), calls=%async_computation.1 | async-start | bytes 3145728 | tf_op jit(solution)/shard_map/all_gather | solution.py:22
  61.3 213.2 %all-gather.10.cloned.1.call-start = ((), (), s32[]{:S(2)}) async-start(), calls=%async_computation.2 | async-start | bytes 35651584 | tf_op jit(solution)/shard_map/all_gather | solution.py:30
  98.6 336.5 %all-gather.12.cloned.1.call-start = ((), (), s32[]{:S(2)}) async-start(), calls=%async_computation.3 | async-start | bytes 8912896 | tf_op jit(solution)/shard_map/all_gather | solution.py:34
  333.9 110.9 %copy-start.3 = (f32[512]{0:T(512)S(1)}, f32[512]{0:T(512)}, u32[]{:S(2)}) copy-start(f32[512]{0:T(512)} %param.9) | copy-start | bytes 6148
  435.2 11.2 %copy-start.2 = (f32[8,1024,512]{1,2,0:T(8,128)S(1)}, f32[8,1024,512]{1,2,0:T(8,128)}, u32[]{:S(2)}) copy-start(f32[8,1024,512]{1,2,0:T(8,128)} %convolution_bitcast_fusion) | copy-start | bytes 50331652
  446.3 97.0 %slice-start = ((s8[8388608]{0:T(1024)(128)(4,1)}), s8[4194304]{0:T(1024)(128)(4,1)S(1)}, s32[]{:S(2)}) async-start(s8[8388608]{0:T(1024)(128)(4,1)} %bitcast.25), calls=%async_computation.4 | async-start | bytes 8388608
  479.2 64.2 %slice-start.1 = ((s8[8388608]{0:T(1024)(128)(4,1)}), s8[4194304]{0:T(1024)(128)(4,1)S(1)}, s32[]{:S(2)}) async-start(s8[8388608]{0:T(1024)(128)(4,1)} %bitcast.25), calls=%async_computation.5 | async-start | bytes 8388608
  579.1 80.7 %copy-start.1 = (f32[16,16]{1,0:T(8,128)S(1)}, f32[16,16]{1,0:T(8,128)}, u32[]{:S(2)}) copy-start(f32[16,16]{1,0:T(8,128)} %param.8) | copy-start | bytes 3076
Sparse Core Ops, SparseCore 0:
  9.7 44.1 all-gather.5
  61.4 31.8 all-gather.7
  98.8 175.7 all-gather.9
  363.1 72.0 all-gather.11
